TPU v7x, 32 devices: a whole 2x2x4 slice. The times are simulated.
32 devices in a mesh: dp: 16 (over z, y, core), mp: 2 (over x).
Axes of the slice: x: 2, y: 2, z: 4, core: 2. Of those that a mesh axis runs over, the one named last changes fastest.
Arguments:
- hidden_in: bfloat16 [8192, 2048], P('dp', 'mp'), may hold values from -6 to 6
- doc_starts: int32 [16, 2], replicated, may hold values from 1 to 511, as said below
- attn_gain: bfloat16 [2048], P('dp'), may hold values from 0.25 to 1.75
- w_query: bfloat16 [2048, 2048], P('dp', 'mp'), may hold values from -0.125 to 0.125
- w_key: bfloat16 [2048, 512], P('dp', 'mp'), may hold values from -0.125 to 0.125
- w_value: bfloat16 [2048, 512], P('dp', 'mp'), may hold values from -0.125 to 0.125
- query_gain: bfloat16 [64], replicated, may hold values from 0.25 to 1.75
- key_gain: bfloat16 [64], replicated, may hold values from 0.25 to 1.75
- w_out: bfloat16 [2048, 2048], P('mp', 'dp'), may hold values from -0.5 to 0.5
- mlp_gain: bfloat16 [2048], P('dp'), may hold values from 0.25 to 1.75
- w_gate: bfloat16 [2048, 8192], P('dp', 'mp'), may hold values from -0.125 to 0.125
- w_up: bfloat16 [2048, 8192], P('dp', 'mp'), may hold values from -0.125 to 0.125
- w_down: bfloat16 [8192, 2048], P('mp', 'dp'), may hold values from -0.125 to 0.125
- cotangent: bfloat16 [8192, 2048], P('dp', 'mp'), may hold values from -12 to 12
Outputs:
- block_out: bfloat16 [8192, 2048], P('dp', 'mp')
- d_input: float32 [8192, 2048], P('dp', 'mp')
- d_attn_gain: float32 [2048], P('dp')
- d_query: float32 [2048, 2048], P('dp', 'mp')
- d_key: float32 [2048, 512], P('dp', 'mp')
- d_value: float32 [2048, 512], P('dp', 'mp')
- d_query_gain: float32 [64], replicated
- d_key_gain: float32 [64], replicated
- d_out_proj: float32 [2048, 2048], P('mp', 'dp')
- d_mlp_gain: float32 [2048], P('dp')
- d_gate: float32 [2048, 8192], P('dp', 'mp')
- d_up: float32 [2048, 8192], P('dp', 'mp')
- d_down: float32 [8192, 2048], P('mp', 'dp')
Inputs may be any that keep to these rules, and one draw needn't show every extreme that they name: `doc_starts`: in each row the first number is at most the second; documents may be empty.
All inputs are finite; a program needn't handle non-finite values.
Results may differ from a plain program's by a relative error of at most 0.017.
Values may be sent and summed in bfloat16 or wider, within the bound.
A program may use at most 256 MiB of HBM per device.

v0:
```python
from functools import partial
import math
import jax
import jax.numpy as jnp
from jax import lax
from jax.sharding import Mesh, PartitionSpec as P

BF = jnp.bfloat16
F32 = jnp.float32
EPS = 1e-05
TP = ("i", "m")
ALL = ("t", "i", "m")


def dot_f32(left, right, dims):
    return lax.dot_general(left, right, (dims, ((), ())), preferred_element_type=F32)


def nn(left, right):
    return dot_f32(left, right, ((1,), (0,)))


def nt(left, right):
    return dot_f32(left, right, ((1,), (1,)))


def tn(left, right):
    return dot_f32(left, right, ((0,), (0,)))


def rms_rows(v, gain):
    return v * lax.rsqrt(jnp.mean(v * v, axis=-1, keepdims=True) + EPS) * gain


def tables(cut_row, length, head_dim):
    position = jnp.arange(length, dtype=jnp.int32)
    doc = (position >= cut_row[0]).astype(jnp.int32) + (position >= cut_row[1]).astype(jnp.int32)
    starts = jnp.where(doc == 0, 0, jnp.where(doc == 1, cut_row[0], cut_row[1]))
    places = (position - starts).astype(F32)
    freqs = jnp.exp(-math.log(1000000.0) * 2.0 * jnp.arange(head_dim // 2, dtype=F32) / head_dim)
    angles = places[:, None] * freqs[None, :]
    angles = jnp.concatenate([angles, angles], axis=-1)
    allowed = (doc[:, None] == doc[None, :]) & (position[None, :] <= position[:, None])
    return (jnp.cos(angles), jnp.sin(angles), allowed)


def rotate(v, cosine, sine_table):
    halfway = v.shape[-1] // 2
    turned = jnp.concatenate([-v[..., halfway:], v[..., :halfway]], axis=-1)
    return v * cosine + turned * sine_table


def head_piece(pre, gain, cosine, sine_table):
    shaped = pre.reshape(pre.shape[0], -1, gain.shape[0])
    return rotate(rms_rows(shaped, gain), cosine, sine_table)


def attend(inputs, scale):
    queries, keys, values, allowed = inputs
    scores = jnp.einsum("qgd,td->gqt", queries, keys, preferred_element_type=F32) * scale
    scores = jnp.where(allowed[None], scores, -1e30)
    highest = jnp.max(scores, axis=-1, keepdims=True)
    weights_exp = jnp.exp(scores - highest)
    totals = jnp.sum(weights_exp, axis=-1, keepdims=True)
    probs = weights_exp / totals
    log_norm = highest[..., 0] + jnp.log(totals[..., 0])
    outputs = jnp.einsum("gqt,td->qgd", probs.astype(BF), values, preferred_element_type=F32)
    return (outputs.astype(BF), log_norm)


def attend_grad(inputs, scale):
    queries, keys, values, d_outputs, log_norm, allowed = inputs
    scores = jnp.einsum("qgd,td->gqt", queries, keys, preferred_element_type=F32) * scale
    scores = jnp.where(allowed[None], scores, -1e30)
    probs = jnp.exp(scores - log_norm[..., None])
    d_probs = jnp.einsum("qgd,td->gqt", d_outputs, values, preferred_element_type=F32)
    inner_sum = jnp.sum(probs * d_probs, axis=-1, keepdims=True)
    d_scores = (probs * (d_probs - inner_sum)).astype(BF)
    d_queries = jnp.einsum("gqt,td->qgd", d_scores, keys, preferred_element_type=F32) * scale
    d_keys = jnp.einsum("gqt,qgd->td", d_scores, queries, preferred_element_type=F32) * scale
    d_values = jnp.einsum("gqt,qgd->td", probs.astype(BF), d_outputs, preferred_element_type=F32)
    return (d_queries, d_keys, d_values)


def gather_pieces(piece, ranks):
    rows, cols = piece.shape
    parts = lax.all_gather(piece, TP, axis=0)
    parts = parts.reshape(ranks[0], ranks[1], rows, cols)
    return jnp.moveaxis(parts, 1, 2).reshape(ranks[0] * rows, ranks[1] * cols)


def scatter_pieces(partial_sum, ranks):
    rows, cols = partial_sum.shape
    parts = partial_sum.astype(BF).reshape(ranks[0], rows // ranks[0], ranks[1], cols // ranks[1])
    parts = jnp.moveaxis(parts, 2, 1).reshape(-1, rows // ranks[0], cols // ranks[1])
    mine = lax.psum_scatter(parts, TP, scatter_dimension=0, tiled=False)
    return mine.astype(F32)


def spread(local, inner):
    rows, cols = local.shape
    parts = jnp.moveaxis(local.reshape(rows, inner, cols // inner), 1, 0)
    parts = lax.all_to_all(parts, "i", 0, 0, tiled=False)
    return parts.reshape(inner * rows, cols // inner)


def collect(block, inner):
    rows, cols = block.shape
    parts = lax.all_to_all(block.reshape(inner, rows // inner, cols), "i", 0, 0, tiled=False)
    return jnp.moveaxis(parts, 0, 1).reshape(rows // inner, inner * cols)


def full_rows(local, inner):
    return lax.all_gather(spread(local, inner), "t", axis=0, tiled=True)


def grad_rows(part, inner):
    mine = lax.psum_scatter(part.astype(BF), "t", scatter_dimension=0, tiled=True)
    return collect(mine, inner).astype(F32)


def body(
    hidden_in,
    doc_starts,
    attn_gain,
    w_query,
    w_key,
    w_value,
    query_gain,
    key_gain,
    w_out,
    mlp_gain,
    w_gate,
    w_up,
    w_down,
    cotangent,
    *,
    groups,
    inner,
    halves
):
    length, width_part = hidden_in.shape
    ranks = (inner, halves)
    width = width_part * halves
    head_dim = query_gain.shape[0]
    scale = head_dim ** (-0.5)
    t_index, m_index = (lax.axis_index("t"), lax.axis_index("m"))
    cuts = lax.dynamic_slice_in_dim(doc_starts, t_index * inner, inner, 0)
    cosine, sine_table, allowed = jax.vmap(partial(tables, length=length, head_dim=head_dim))(cuts)
    cosine = cosine.reshape(inner * length, 1, head_dim)
    sine_table = sine_table.reshape(inner * length, 1, head_dim)
    q_gain, k_gain = (query_gain.astype(F32), key_gain.astype(F32))
    gains = lax.all_gather(jnp.stack([attn_gain, mlp_gain], 1), ("t", "i"), axis=0, tiled=True)
    gain_one, gain_two = (gains[:, 0].astype(F32), gains[:, 1].astype(F32))
    full_in = gather_pieces(hidden_in, ranks)
    sizes = [w.shape[1] // inner for w in (w_query, w_key, w_value)] + [w_out.shape[0] // inner]
    edges = [sum(sizes[:n]) for n in range(5)]

    def by_rank(w):
        return w.reshape(w.shape[0], inner, w.shape[1] // inner)

    attn_local = jnp.concatenate(
        [by_rank(w_query), by_rank(w_key), by_rank(w_value), by_rank(w_out.T)], 2
    )
    attn_cols = full_rows(attn_local.reshape(attn_local.shape[0], -1), inner)
    query_cols, key_cols, value_cols, out_t = [
        attn_cols[:, edges[n] : edges[n + 1]] for n in range(4)
    ]
    resid = full_in.astype(F32)
    r_one = lax.rsqrt(jnp.mean(resid * resid, axis=-1, keepdims=True) + EPS)
    normed_one = (resid * r_one * gain_one).astype(BF)
    gate_cols = full_rows(w_gate, inner)
    up_cols = full_rows(w_up, inner)
    down_t = full_rows(w_down.T, inner)
    grad_full = gather_pieces(cotangent, ranks)
    query_pre = nn(normed_one, query_cols)
    key_pre = nn(normed_one, key_cols)
    value_low = nn(normed_one, value_cols).astype(BF)
    query_rot = head_piece(query_pre, q_gain, cosine, sine_table).astype(BF)
    key_rot = head_piece(key_pre, k_gain, cosine, sine_table).astype(BF)
    group = query_rot.shape[1]
    query_stack = query_rot.reshape(inner, length, group, head_dim)
    key_stack = key_rot.reshape(inner, length, head_dim)
    value_stack = value_low.reshape(inner, length, head_dim)
    attended, log_norm = lax.map(
        partial(attend, scale=scale), (query_stack, key_stack, value_stack, allowed)
    )
    mixed = attended.reshape(inner * length, group * head_dim)
    middle = hidden_in.astype(F32) + scatter_pieces(nt(mixed, out_t), ranks)
    my_gain_one = lax.dynamic_slice_in_dim(gain_one, m_index * width_part, width_part, 0)
    my_gain_two = lax.dynamic_slice_in_dim(gain_two, m_index * width_part, width_part, 0)
    r_two = lax.rsqrt(lax.psum(jnp.sum(middle * middle, axis=-1, keepdims=True), "m") / width + EPS)
    normed_two = gather_pieces((middle * r_two * my_gain_two).astype(BF), ranks)
    gate_pre, up_pre = (nn(normed_two, gate_cols), nn(normed_two, up_cols))
    d_inner = nn(grad_full, down_t)
    sigmoid_gate = jax.nn.sigmoid(gate_pre)
    inner_act = (gate_pre * sigmoid_gate * up_pre).astype(BF)
    d_gate_pre = (d_inner * up_pre * sigmoid_gate * (1.0 + gate_pre * (1.0 - sigmoid_gate))).astype(
        BF
    )
    d_up_pre = (d_inner * gate_pre * sigmoid_gate).astype(BF)
    d_normed_two = scatter_pieces(nt(d_gate_pre, gate_cols) + nt(d_up_pre, up_cols), ranks)
    mlp_out = scatter_pieces(nt(inner_act, down_t), ranks)
    block_out = (middle + mlp_out).astype(BF)
    scaled = d_normed_two * my_gain_two
    dot_two = lax.psum(jnp.sum(scaled * middle, axis=-1, keepdims=True), "m") / width
    d_gain_two = jnp.sum(d_normed_two * middle * r_two, axis=0)
    d_middle = cotangent.astype(F32) + r_two * scaled - middle * (r_two * r_two * r_two) * dot_two
    d_middle_low = gather_pieces(d_middle.astype(BF), ranks)
    d_gate = grad_rows(tn(normed_two, d_gate_pre), inner)
    d_up = grad_rows(tn(normed_two, d_up_pre), inner)
    d_down = grad_rows(tn(grad_full, inner_act), inner).T
    d_mixed = nn(d_middle_low, out_t).astype(BF)
    d_out_part = tn(d_middle_low, mixed)
    d_mixed_stack = d_mixed.reshape(inner, length, group, head_dim)
    d_query_stack, d_key_stack, d_value_stack = lax.map(
        partial(attend_grad, scale=scale),
        (query_stack, key_stack, value_stack, d_mixed_stack, log_norm, allowed),
    )
    rotary_piece = partial(head_piece, cosine=cosine, sine_table=sine_table)
    _, query_pull = jax.vjp(rotary_piece, query_pre, q_gain)
    d_query_pre, d_qgain_part = query_pull(d_query_stack.reshape(inner * length, group, head_dim))
    _, key_pull = jax.vjp(rotary_piece, key_pre, k_gain)
    d_key_pre, d_kgain_part = key_pull(d_key_stack.reshape(inner * length, 1, head_dim))
    d_heads = jnp.concatenate(
        [d_query_pre, d_key_pre, d_value_stack.reshape(inner * length, head_dim)], 1
    ).astype(BF)
    heads_cols = attn_cols[:, : edges[3]]
    d_normed_one = scatter_pieces(nt(d_heads, heads_cols), ranks)
    d_attn = jnp.concatenate([tn(normed_one, d_heads), d_out_part], 1)
    d_attn = grad_rows(d_attn, inner).reshape(-1, inner, edges[4])
    d_query, d_key, d_value, d_out_t = [
        d_attn[:, :, edges[n] : edges[n + 1]].reshape(d_attn.shape[0], -1) for n in range(4)
    ]
    mine = hidden_in.astype(F32)
    i_index = lax.axis_index("i")
    r_own = lax.dynamic_slice_in_dim(r_one, i_index * length, length, 0)
    scaled = d_normed_one * my_gain_one
    dot_one = lax.psum(jnp.sum(scaled * mine, axis=-1, keepdims=True), "m") / width
    d_gain_one = jnp.sum(d_normed_one * mine * r_own, axis=0)
    d_input = d_middle + r_own * scaled - mine * (r_own * r_own * r_own) * dot_one
    both = jnp.stack([d_gain_one, d_gain_two], 0)
    wide = lax.dynamic_update_slice(jnp.zeros((2, width), F32), both, (0, m_index * width_part))
    small = jnp.concatenate([wide.reshape(-1), d_qgain_part, d_kgain_part])
    small = lax.psum(small, ALL)
    wide = small[: 2 * width].reshape(2, width)
    shard = attn_gain.shape[0]
    own = lax.dynamic_slice(wide, (0, (t_index * inner + i_index) * shard), (2, shard))
    return (
        block_out,
        d_input,
        own[0],
        d_query,
        d_key,
        d_value,
        small[2 * width : 2 * width + head_dim],
        small[2 * width + head_dim :],
        d_out_t.T,
        own[1],
        d_gate,
        d_up,
        d_down,
    )


def solution(mesh):
    dp, halves = (mesh.shape["dp"], mesh.shape["mp"])
    inner = 4
    groups = dp // inner
    fine = Mesh(mesh.devices.reshape(groups, inner, halves), ("t", "i", "m"))
    rows = P(("t", "i"))
    block = P(("t", "i"), "m")
    turned = P("m", ("t", "i"))
    return jax.shard_map(
        partial(body, groups=groups, inner=inner, halves=halves),
        mesh=fine,
        in_specs=(
            block,
            P(),
            rows,
            block,
            block,
            block,
            P(),
            P(),
            turned,
            rows,
            block,
            block,
            turned,
            block,
        ),
        out_specs=(
            block,
            block,
            rows,
            block,
            block,
            block,
            P(),
            P(),
            turned,
            rows,
            block,
            block,
            turned,
        ),
        check_vma=False,
    )
```

profile of v0, /device:TPU:0, one launch (start us, length us, event | category | flops | bytes accessed | tf_op | source)
XLA Modules:
  0.0 1419.3 jit_solution(7471907104294036596)
XLA Ops:
  11.3 14.3 %all_to_all.40 = bf16[4,128,640]{1,2,0:T(8,128)(2,1)S(1)} all-to-all(bf16[4,128,640]{1,2,0:T(8,128)(2,1)S(1)} %maximum_bitcast_fusion), channel_id=1, replica_groups=mesh['t'=4,'i'=4,'m'=2] {'i'}, dimensions={0} | all-to-all | bytes 1310720 | tf_op jit(solution)/shard_map/all_to_all | solution.py:103
  27.7 20.5 %all_gather.41 = bf16[2048,2]{0,1:T(2,128)(2,1)S(1)} all-gather(bf16[128,2]{0,1:T(2,128)(2,1)S(1)} %pad_maximum_fusion.6), channel_id=1, replica_groups=mesh['t'=4,'i'=4,'m'=2] {'t','i'}, dimensions={0}, use_global_device_ids=true | all-gather | bytes 8704 | tf_op jit(solution)/shard_map/all_gather | solution.py:153
  50.1 31.7 %all-gather.13.cloned.1.call-done = bf16[2048,640]{0,1:T(8,128)(2,1)} async-done(((bf16[512,640]{0,1:T(8,128)(2,1)}), bf16[2048,640]{0,1:T(8,128)(2,1)}) %all-gather.13.cloned.1.call-update) | async-done | bytes 2621456 | tf_op jit(solution)/shard_map/all_gather | solution.py:114
  81.8 55.0 %all-gather.21.cloned.1.call-done = bf16[4096,1024]{1,0:T(8,128)(2,1)} async-done(((bf16[512,1024]{1,0:T(8,128)(2,1)}), bf16[4096,1024]{1,0:T(8,128)(2,1)}) %all-gather.21.cloned.1.call-update) | async-done | bytes 8388624 | tf_op jit(solution)/shard_map/all_gather | solution.py:87
  142.5 11.3 bitcast_convert_fusion
  153.9 27.7 %copy.137 = f32[4,2,512,1024]{3,1,2,0:T(2,128)S(1)} copy(f32[4,2,512,1024]{3,2,1,0:T(8,128)} %bitcast_convert_fusion) | data formatting | bytes 33554432 | tf_op jit(solution)/shard_map/convert_element_type | solution.py:169
  203.6 16.4 %copy.142 = bf16[4,512,2,1024]{3,2,1,0:T(2,128)(2,1)} copy(bf16[4,512,2,1024]{3,1,2,0:T(8,128)(2,1)} %fusion.58) | data formatting | bytes 16777216 | tf_op jit(solution)/shard_map/mul | solution.py:171
  220.1 14.8 %reshape.761 = bf16[2048,2048,1]{1,0,2:T(8,128)(2,1)} reshape(bf16[4,512,2,1024]{3,2,1,0:T(2,128)(2,1)} %copy.142) | data formatting | bytes 16777216 | tf_op jit(solution)/shard_map/convert_element_type | solution.py:171
  250.3 18.6 %while.26 = (s32[]{:T(128)}, bf16[4,512,4,64]{1,3,2,0:T(8,128)(2,1)}, f32[4,4,512]{2,1,0:T(4,128)}, bf16[4,512,64]{1,2,0:T(8,128)(2,1)S(1)}, pred[4,512,512]{1,2...) while((s32[]{:T(128)}, ...), condition=%wide.region_6.7_spmd, body=%wide.region_3.6_spmd.sunk | while | flops 281147392 | bytes 14617177 | solution.py:185
  278.9 14.5 %reshape.696 = bf16[4,512,2,1024]{3,2,1,0:T(2,128)(2,1)} reshape(bf16[2048,2048]{1,0:T(8,128)(2,1)} %convolution_convert_fusion.2) | data formatting | bytes 16777216 | tf_op jit(solution)/shard_map/reshape | solution.py:94
  303.4 70.8 %reduce-scatter.9.cloned.1.call-done = bf16[1,512,1024]{2,1,0:T(8,128)(2,1)} async-done(((bf16[8,512,1024]{2,1,0:T(8,128)(2,1)}), bf16[1,512,1024]{2,1,0:T(8,128)(2,1)}) %reduce-scatter.9.cloned.1.call-update) | async-done | bytes 1048592 | tf_op jit(solution)/shard_map/reduce_scatter | solution.py:96
  384.2 25.4 %all_to_all.41 = bf16[4,128,1024]{1,2,0:T(8,128)(2,1)S(1)} all-to-all(bf16[4,128,1024]{1,2,0:T(8,128)(2,1)S(1)} %bitcast.453), channel_id=1, replica_groups=mesh['t'=4,'i'=4,'m'=2] {'i'}, dimensions={0} | all-to-all | bytes 2097152 | tf_op jit(solution)/shard_map/all_to_all | solution.py:103
  412.6 28.4 %all_to_all.42 = bf16[4,128,1024]{1,2,0:T(8,128)(2,1)S(1)} all-to-all(bf16[4,128,1024]{1,2,0:T(8,128)(2,1)S(1)} %bitcast.454), channel_id=1, replica_groups=mesh['t'=4,'i'=4,'m'=2] {'i'}, dimensions={0} | all-to-all | bytes 2097152 | tf_op jit(solution)/shard_map/all_to_all | solution.py:103
  442.4 18.0 %all_to_all.43 = bf16[4,128,1024]{1,2,0:T(8,128)(2,1)S(1)} all-to-all(bf16[4,128,1024]{1,2,0:T(8,128)(2,1)} %bitcast.462), channel_id=1, replica_groups=mesh['t'=4,'i'=4,'m'=2] {'i'}, dimensions={0} | all-to-all | bytes 2097152 | tf_op jit(solution)/shard_map/all_to_all | solution.py:103
  461.8 16.7 %copy.155 = bf16[4,2,512,1024]{3,1,2,0:T(2,128)(2,1)} copy(bf16[4,2,512,1024]{3,2,1,0:T(8,128)(2,1)} %bitcast.439) | data formatting | bytes 16777216 | tf_op jit(solution)/shard_map/reshape | solution.py:88
  478.5 10.9 copy.217
  489.4 18.2 %all-gather.23.cloned.1.call-done = bf16[4096,1024]{1,0:T(8,128)(2,1)} async-done(((bf16[512,1024]{1,0:T(8,128)(2,1)}), bf16[4096,1024]{1,0:T(8,128)(2,1)}) %all-gather.23.cloned.1.call-update) | async-done | bytes 8388624 | tf_op jit(solution)/shard_map/all_gather | solution.py:87
  507.5 16.4 %copy.148 = bf16[4,2,512,1024]{3,1,2,0:T(2,128)(2,1)} copy(bf16[4,2,512,1024]{3,2,1,0:T(8,128)(2,1)} %bitcast.444) | data formatting | bytes 16777216 | tf_op jit(solution)/shard_map/reshape | solution.py:88
  534.2 56.2 %all-gather.15.cloned.1.call-done = bf16[2048,1024]{1,0:T(8,128)(2,1)} async-done(((bf16[512,1024]{1,0:T(8,128)(2,1)}), bf16[2048,1024]{1,0:T(8,128)(2,1)}) %all-gather.15.cloned.1.call-update) | async-done | bytes 4194320 | tf_op jit(solution)/shard_map/all_gather | solution.py:114
  590.4 14.7 %fusion.116 = f32[2048,1024]{1,0:T(8,128)} fusion(bf16[2048,2048]{1,0:T(8,128)(2,1)} %bitcast.440, bf16[2048,1024]{1,0:T(8,128)(2,1)} %all-gather.15.cloned.1.call-done), kind=kOutput, calls=%fused_computation.219 | convolution fusion | flops 8589934592 | bytes 20971520 | tf_op jit(solution)/shard_map/dot_general | solution.py:16
  605.1 66.3 %all-gather.17.cloned.1.call-done = bf16[2048,1024]{1,0:T(8,128)(2,1)} async-done(((bf16[512,1024]{1,0:T(8,128)(2,1)}), bf16[2048,1024]{1,0:T(8,128)(2,1)}) %all-gather.17.cloned.1.call-update) | async-done | bytes 4194320 | tf_op jit(solution)/shard_map/all_gather | solution.py:114
  671.4 14.4 %fusion.117 = f32[2048,1024]{1,0:T(8,128)} fusion(bf16[2048,2048]{1,0:T(8,128)(2,1)} %bitcast.441, bf16[2048,1024]{1,0:T(8,128)(2,1)} %all-gather.17.cloned.1.call-done), kind=kOutput, calls=%fused_computation.220 | convolution fusion | flops 8589934592 | bytes 20971520 | tf_op jit(solution)/shard_map/dot_general | solution.py:16
  685.8 66.6 %all-gather.19.cloned.1.call-done = bf16[2048,1024]{1,0:T(8,128)(2,1)} async-done(((bf16[512,1024]{1,0:T(8,128)(2,1)}), bf16[2048,1024]{1,0:T(8,128)(2,1)}) %all-gather.19.cloned.1.call-update) | async-done | bytes 4194320 | tf_op jit(solution)/shard_map/all_gather | solution.py:114
  752.4 21.8 %multiply_convert_fusion.2 = (bf16[2048,1024]{1,0:T(8,128)(2,1)}, bf16[2048,1024]{1,0:T(8,128)(2,1)}, bf16[2048,1024]{1,0:T(8,128)(2,1)}) fusion(f32[2048,1024]{1,0:T(8,128)} %fusion.116, f32[2048,1024]{1,0:T(8,128)} %fusion.117, bf16[2048,2048]{1,0:T(8,128)(2,1)} %bitcast.437, bf16[2048,1024]{1,0:T(8,128)(2,1)} %all-gather.19.cloned.1.call-done), kind=kOutput, calls=%fused_computation.70 | convolution fusion | flops 8623489024 | bytes 41943040 | tf_op jit(solution)/shard_map/dot_general | solution.py:16
  774.2 14.4 %fusion.118 = f32[2048,2048]{1,0:T(8,128)} fusion(bf16[2048,1024]{1,0:T(8,128)(2,1)} %get-tuple-element.270, bf16[2048,1024]{1,0:T(8,128)(2,1)S(1)} %copy-done.62), kind=kOutput, calls=%fused_computation.221 | convolution fusion | flops 8589934592 | bytes 25165824 | tf_op jit(solution)/shard_map/dot_general | solution.py:16
  788.6 16.4 %add_convert_fusion = bf16[2048,2048]{1,0:T(8,128)(2,1)} fusion(f32[2048,2048]{1,0:T(8,128)} %fusion.118, bf16[2048,1024]{1,0:T(8,128)(2,1)} %get-tuple-element.269, bf16[2048,1024]{1,0:T(8,128)(2,1)} %all-gather.17.cloned.1.call-done), kind=kOutput, calls=%fused_computation.65 | convolution fusion | flops 8598323200 | bytes 33554432 | tf_op jit(solution)/shard_map/dot_general | solution.py:16
  805.0 14.5 %reshape.710 = bf16[4,512,2,1024]{3,2,1,0:T(2,128)(2,1)} reshape(bf16[2048,2048]{1,0:T(8,128)(2,1)} %add_convert_fusion) | data formatting | bytes 16777216 | tf_op jit(solution)/shard_map/reshape | solution.py:94
  828.9 69.9 %reduce-scatter.13.cloned.1.call-done = bf16[1,512,1024]{2,1,0:T(8,128)(2,1)} async-done(((bf16[8,512,1024]{2,1,0:T(8,128)(2,1)}), bf16[1,512,1024]{2,1,0:T(8,128)(2,1)}) %reduce-scatter.13.cloned.1.call-update) | async-done | bytes 1048592 | tf_op jit(solution)/shard_map/reduce_scatter | solution.py:96
  910.4 14.0 convolution_convert_fusion.3
  924.5 14.0 convolution_convert_fusion.4
  938.8 14.5 %convert_bitcast_fusion = bf16[2048,1024]{0,1:T(8,128)(2,1)} fusion(bf16[2048,1024]{1,0:T(8,128)(2,1)} %get-tuple-element.271, bf16[2048,2048]{1,0:T(8,128)(2,1)} %bitcast.438), kind=kOutput, calls=%fused_computation.77 | convolution fusion | flops 8592031744 | bytes 16777216 | tf_op jit(solution)/shard_map/dot_general | solution.py:16
  953.3 11.5 all-gather.27.cloned.1.call-done
  964.9 16.4 %copy.157 = bf16[4,2,512,1024]{3,1,2,0:T(2,128)(2,1)} copy(bf16[4,2,512,1024]{3,2,1,0:T(8,128)(2,1)} %bitcast.445) | data formatting | bytes 16777216 | tf_op jit(solution)/shard_map/reshape | solution.py:88
  981.3 10.5 copy.219
  1004.3 116.4 %while.27 = (s32[]{:T(128)}, f32[4,512,4,64]{1,0,3,2:T(4,128)}, f32[4,512,64]{1,0,2:T(4,128)}, bf16[4,512,64]{1,2,0:T(8,128)(2,1)}, bf16[4,512,64]{1,2,0:T(8,128...) while((s32[]{:T(128)}, f32[4,512,4,64]{1,0,3,2:T(4,128)}, ...), condition=%wide.region_16.17_spmd, body=%wide.region_14.16_spmd.sunk | while | flops 686979072 | bytes 54259364 | solution.py:216
  1013.1 11.1 dynamic_update_slice.35
  1042.1 11.1 dynamic_update_slice.35
  1071.0 11.1 dynamic_update_slice.35
  1100.0 11.1 dynamic_update_slice.35
  1154.6 14.5 %reshape.721 = bf16[4,512,2,1024]{3,2,1,0:T(2,128)(2,1)} reshape(bf16[2048,2048]{1,0:T(8,128)(2,1)} %convolution_convert_fusion) | data formatting | bytes 16777216 | tf_op jit(solution)/shard_map/reshape | solution.py:94
  1178.5 14.2 %convolution_convert_fusion.1 = bf16[2048,2048]{1,0:T(8,128)(2,1)} fusion(bf16[2048,1024]{1,0:T(8,128)(2,1)} %get-tuple-element.271, bf16[2048,1024]{1,0:T(8,128)(2,1)} %all-gather.19.cloned.1.call-done), kind=kOutput, calls=%fused_computation.75 | convolution fusion | flops 8594128896 | bytes 16777216 | tf_op jit(solution)/shard_map/dot_general | solution.py:16
  1192.8 14.5 %reshape.706 = bf16[4,512,2,1024]{3,2,1,0:T(2,128)(2,1)} reshape(bf16[2048,2048]{1,0:T(8,128)(2,1)} %convolution_convert_fusion.1) | data formatting | bytes 16777216 | tf_op jit(solution)/shard_map/reshape | solution.py:94
  1220.4 14.4 %all-to-all-done.6 = bf16[4,128,1024]{2,1,0:T(8,128)(2,1)S(1)} async-done(((bf16[4,128,1024]{2,1,0:T(8,128)(2,1)}), bf16[4,128,1024]{2,1,0:T(8,128)(2,1)S(1)}, u32[]{:S(2)}, u32[]{:S(2)}) %all-to-all-start.6) | async-done | bytes 1048608 | tf_op jit(solution)/shard_map/all_to_all | solution.py:109
  1240.7 12.0 all-to-all-done.5
  1260.1 10.6 all-to-all-done.7
  1293.1 39.7 %reduce-scatter.15.cloned.1.call-done = bf16[1,512,1024]{2,1,0:T(8,128)(2,1)} async-done(((bf16[8,512,1024]{2,1,0:T(8,128)(2,1)}), bf16[1,512,1024]{2,1,0:T(8,128)(2,1)}) %reduce-scatter.15.cloned.1.call-update) | async-done | bytes 1048592 | tf_op jit(solution)/shard_map/reduce_scatter | solution.py:96
  1335.0 39.7 %psum.31 = f32[4224]{0:T(1024)S(1)} all-reduce(f32[4224]{0:T(1024)S(1)} %concatenate.65), channel_id=1, replica_groups=mesh['t'=4,'i'=4,'m'=2] {'t','i','m'}, use_global_device_ids=true, to_apply=%region_26.27 | all-reduce | flops 4224 | bytes 33792 | tf_op jit(solution)/shard_map/psum | solution.py:245
  1381.1 26.9 %reduce-scatter.11.cloned.1.call-done = bf16[1,512,1024]{2,1,0:T(8,128)(2,1)} async-done(((bf16[8,512,1024]{2,1,0:T(8,128)(2,1)}), bf16[1,512,1024]{2,1,0:T(8,128)(2,1)}) %reduce-scatter.11.cloned.1.call-update) | async-done | bytes 1048592 | tf_op jit(solution)/shard_map/reduce_scatter | solution.py:96
  (381 shorter events, 324.6 us)
Async XLA Ops:
  7.2 20.2 %copy-start = (s32[16,2]{0,1:T(2,128)S(1)}, s32[16,2]{0,1:T(2,128)}, u32[]{:S(2)}) copy-start(s32[16,2]{0,1:T(2,128)} %param.19) | copy-start | bytes 388
  7.2 20.4 %copy-start.63 = (bf16[64]{0:T(256)(128)(2,1)S(1)}, bf16[64]{0:T(256)(128)(2,1)}, u32[]{:S(2)}) copy-start(bf16[64]{0:T(256)(128)(2,1)} %param.25) | copy-start | bytes 388
  7.2 20.4 %copy-start.65 = (bf16[128]{0:T(256)(128)(2,1)S(1)}, bf16[128]{0:T(256)(128)(2,1)}, u32[]{:S(2)}) copy-start(bf16[128]{0:T(256)(128)(2,1)} %param.20) | copy-start | bytes 772
  7.2 20.4 %copy-start.64 = (bf16[128]{0:T(256)(128)(2,1)S(1)}, bf16[128]{0:T(256)(128)(2,1)}, u32[]{:S(2)}) copy-start(bf16[128]{0:T(256)(128)(2,1)} %param.27) | copy-start | bytes 772
  7.2 40.9 %copy-start.66 = (bf16[64]{0:T(256)(128)(2,1)S(1)}, bf16[64]{0:T(256)(128)(2,1)}, u32[]{:S(2)}) copy-start(bf16[64]{0:T(256)(128)(2,1)} %param.24) | copy-start | bytes 388
  7.2 74.5 %all-gather.13.cloned.1.call-start = ((), (), s32[]{:S(2)}) async-start(), calls=%async_computation.16 | async-start | bytes 3276800 | tf_op jit(solution)/shard_map/all_gather | solution.py:114
  26.6 110.3 %all-gather.21.cloned.1.call-start = ((), (), s32[]{:S(2)}) async-start(), calls=%async_computation.28 | async-start | bytes 9437184 | tf_op jit(solution)/shard_map/all_gather | solution.py:87
  27.3 346.9 %reduce-scatter.9.cloned.1.call-start = ((), (), s32[]{:S(2)}) async-start(), calls=%async_computation.17 | async-start | bytes 9437184 | tf_op jit(solution)/shard_map/reduce_scatter | solution.py:96
  27.6 213.8 %copy-start.60 = (f32[64]{0:T(128)}, f32[64]{0:T(128)S(1)}, u32[]{:S(2)}) copy-start(f32[64]{0:T(128)S(1)} %convert_element_type.239) | copy-start | bytes 772
  48.2 196.1 %copy-start.58 = (f32[64]{0:T(128)}, f32[64]{0:T(128)S(1)}, u32[]{:S(2)}) copy-start(f32[64]{0:T(128)S(1)} %convert_element_type.247) | copy-start | bytes 772
  49.2 138.4 %copy-start.48 = (f32[2048,1]{0,1:T(1,128)}, f32[2048,1]{0,1:T(1,128)S(1)}, u32[]{:S(2)}) copy-start(f32[2048,1]{0,1:T(1,128)S(1)} %get-tuple-element.297) | copy-start | bytes 24580
  193.4 48.0 %copy-start.11 = (f32[2048,64]{0,1:T(8,128)}, f32[2048,64]{0,1:T(8,128)S(1)}, u32[]{:S(2)}) copy-start(f32[2048,64]{0,1:T(8,128)S(1)} %get-tuple-element.306) | copy-start | bytes 1572868
  194.0 47.4 %copy-start.40 = (f32[2048]{0:T(1024)}, f32[2048]{0:T(1024)S(1)}, u32[]{:S(2)}) copy-start(f32[2048]{0:T(1024)S(1)} %fusion.102) | copy-start | bytes 24580
  302.7 71.5 %copy-start.4 = (bf16[512,1024]{1,0:T(8,128)(2,1)S(1)}, bf16[512,1024]{1,0:T(8,128)(2,1)}, u32[]{:S(2)}) copy-start(bf16[512,1024]{1,0:T(8,128)(2,1)} %param.18) | copy-start | bytes 3145732
  302.7 80.8 %copy-start.32 = (bf16[128,4096]{1,0:T(8,128)(2,1)S(1)}, bf16[128,4096]{1,0:T(8,128)(2,1)}, u32[]{:S(2)}) copy-start(bf16[128,4096]{1,0:T(8,128)(2,1)} %param.28) | copy-start | bytes 3145732
  302.7 159.0 %all-gather.25.cloned.1.call-start = ((), (), s32[]{:S(2)}) async-start(), calls=%async_computation.30 | async-start | bytes 9437184 | tf_op jit(solution)/shard_map/all_gather | solution.py:87
  303.3 204.2 %all-gather.23.cloned.1.call-start = ((), (), s32[]{:S(2)}) async-start(), calls=%async_computation.29 | async-start | bytes 9437184 | tf_op jit(solution)/shard_map/all_gather | solution.py:87
  303.4 603.3 %copy-start.44 = (f32[1024,1]{0,1:T(1,128)}, f32[1024,1]{0,1:T(1,128)S(1)}, u32[]{:S(2)}) copy-start(f32[1024,1]{0,1:T(1,128)S(1)} %dynamic-slice_convert_fusion) | copy-start | bytes 12292
  380.8 525.9 %copy-start.50 = (f32[512,1]{0,1:T(1,128)}, f32[512,1]{0,1:T(1,128)S(1)}, u32[]{:S(2)}) copy-start(f32[512,1]{0,1:T(1,128)S(1)} %get-tuple-element.264) | copy-start | bytes 6148
  380.8 525.9 %copy-start.53 = (f32[512,1]{0,1:T(1,128)}, f32[512,1]{0,1:T(1,128)S(1)}, u32[]{:S(2)}) copy-start(f32[512,1]{0,1:T(1,128)S(1)} %get-tuple-element.263) | copy-start | bytes 6148
  383.4 207.0 %all-gather.15.cloned.1.call-start = ((), (), s32[]{:S(2)}) async-start(), calls=%async_computation.18 | async-start | bytes 5242880 | tf_op jit(solution)/shard_map/all_gather | solution.py:114
  410.9 260.5 %all-gather.17.cloned.1.call-start = ((), (), s32[]{:S(2)}) async-start(), calls=%async_computation.19 | async-start | bytes 5242880 | tf_op jit(solution)/shard_map/all_gather | solution.py:114
  442.3 310.0 %all-gather.19.cloned.1.call-start = ((), (), s32[]{:S(2)}) async-start(), calls=%async_computation.20 | async-start | bytes 5242880 | tf_op jit(solution)/shard_map/all_gather | solution.py:114
  461.7 437.2 %reduce-scatter.13.cloned.1.call-start = ((), (), s32[]{:S(2)}) async-start(), calls=%async_computation.22 | async-start | bytes 9437184 | tf_op jit(solution)/shard_map/reduce_scatter | solution.py:96
  752.4 21.8 %copy-start.62 = (bf16[2048,1024]{1,0:T(8,128)(2,1)S(1)}, bf16[2048,1024]{1,0:T(8,128)(2,1)}, u32[]{:S(2)}) copy-start(bf16[2048,1024]{1,0:T(8,128)(2,1)} %all-gather.15.cloned.1.call-done) | copy-start | bytes 12582916
  828.8 70.0 %copy-start.8 = (bf16[1,512,1024]{2,1,0:T(8,128)(2,1)S(1)}, bf16[1,512,1024]{2,1,0:T(8,128)(2,1)}, u32[]{:S(2)}) copy-start(bf16[1,512,1024]{2,1,0:T(8,128)(2,1)} %reduce-scatter.9.cloned.1.call-done) | copy-start | bytes 3145732
  828.8 78.4 %copy-start.14 = (bf16[512,1024]{1,0:T(8,128)(2,1)S(1)}, bf16[512,1024]{1,0:T(8,128)(2,1)}, u32[]{:S(2)}) copy-start(bf16[512,1024]{1,0:T(8,128)(2,1)} %param.31) | copy-start | bytes 3145732
  828.9 136.0 %all-gather.27.cloned.1.call-start = ((), (), s32[]{:S(2)}) async-start(), calls=%async_computation.31 | async-start | bytes 9437184 | tf_op jit(solution)/shard_map/all_gather | solution.py:87
  910.3 306.3 %reduce-scatter.21.cloned.1.call-start = ((), (), s32[]{:S(2)}) async-start(), calls=%async_computation.26 | async-start | bytes 5242880 | tf_op jit(solution)/shard_map/reduce_scatter | solution.py:118
  924.5 295.9 %reduce-scatter.19.cloned.1.call-start = ((), (), s32[]{:S(2)}) async-start(), calls=%async_computation.25 | async-start | bytes 5242880 | tf_op jit(solution)/shard_map/reduce_scatter | solution.py:118
  938.5 299.8 %reduce-scatter.23.cloned.1.call-start = ((), (), s32[]{:S(2)}) async-start(), calls=%async_computation.27 | async-start | bytes 5242880 | tf_op jit(solution)/shard_map/reduce_scatter | solution.py:118
  953.3 304.8 %reduce-scatter.17.cloned.1.call-start = ((), (), s32[]{:S(2)}) async-start(), calls=%async_computation.24 | async-start | bytes 3276800 | tf_op jit(solution)/shard_map/reduce_scatter | solution.py:118
  1145.6 187.2 %reduce-scatter.15.cloned.1.call-start = ((), (), s32[]{:S(2)}) async-start(), calls=%async_computation.23 | async-start | bytes 9437184 | tf_op jit(solution)/shard_map/reduce_scatter | solution.py:96
  1178.5 229.5 %reduce-scatter.11.cloned.1.call-start = ((), (), s32[]{:S(2)}) async-start(), calls=%async_computation.21 | async-start | bytes 9437184 | tf_op jit(solution)/shard_map/reduce_scatter | solution.py:96
  1216.7 39.6 %copy-start.49 = (f32[2048,1]{0,1:T(1,128)S(1)}, f32[2048,1]{0,1:T(1,128)}, u32[]{:S(2)}) copy-start(f32[2048,1]{0,1:T(1,128)} %copy-done.48) | copy-start | bytes 24580
  1216.7 39.6 %copy-start.52 = (f32[1,1,4,512]{3,2,1,0:T(4,128)S(1)}, f32[1,1,4,512]{3,2,1,0:T(4,128)}, u32[]{:S(2)}) copy-start(f32[1,1,4,512]{3,2,1,0:T(4,128)} %get-tuple-element.293) | copy-start | bytes 24580
  1216.7 18.1 %all-to-all-start.6 = ((bf16[4,128,1024]{2,1,0:T(8,128)(2,1)}), bf16[4,128,1024]{2,1,0:T(8,128)(2,1)S(1)}, u32[]{:S(2)}, u32[]{:S(2)}) async-start(bf16[4,128,1024]{2,1,0:T(8,128)(2,1)} %bitcast.464), calls=%async_computation.13 | async-start | bytes 2097152 | tf_op jit(solution)/shard_map/all_to_all | solution.py:109
  1234.8 18.0 %all-to-all-start.5 = ((bf16[4,128,1024]{2,1,0:T(8,128)(2,1)}), bf16[4,128,1024]{2,1,0:T(8,128)(2,1)S(1)}, u32[]{:S(2)}, u32[]{:S(2)}) async-start(bf16[4,128,1024]{2,1,0:T(8,128)(2,1)} %bitcast.463), calls=%async_computation.11 | async-start | bytes 2097152 | tf_op jit(solution)/shard_map/all_to_all | solution.py:109
  1252.7 18.0 %all-to-all-start.7 = ((bf16[4,128,1024]{1,2,0:T(8,128)(2,1)}), bf16[4,128,1024]{1,2,0:T(8,128)(2,1)S(1)}, u32[]{:S(2)}, u32[]{:S(2)}) async-start(bf16[4,128,1024]{1,2,0:T(8,128)(2,1)} %copy_bitcast_fusion), calls=%async_computation.15 | async-start | bytes 2097152 | tf_op jit(solution)/shard_map/all_to_all | solution.py:109
  1270.7 14.5 %all-to-all-start.4 = ((bf16[4,128,640]{1,2,0:T(8,128)(2,1)}), bf16[4,128,640]{1,2,0:T(8,128)(2,1)}, u32[]{:S(2)}, u32[]{:S(2)}) async-start(bf16[4,128,640]{1,2,0:T(8,128)(2,1)} %copy_bitcast_fusion.3), calls=%async_computation.9 | async-start | bytes 1310720 | tf_op jit(solution)/shard_map/all_to_all | solution.py:109
  1278.4 54.4 %copy-start.5 = (bf16[512,1024]{1,0:T(8,128)(2,1)S(1)}, bf16[512,1024]{1,0:T(8,128)(2,1)}, u32[]{:S(2)}) copy-start(bf16[512,1024]{1,0:T(8,128)(2,1)} %param.18) | copy-start | bytes 3145732
  1279.8 55.1 %copy-start.57 = (f32[1024]{0:T(1024)S(1)}, f32[1024]{0:T(1024)}, u32[]{:S(2)}) copy-start(f32[1024]{0:T(1024)} %get-tuple-element.219) | copy-start | bytes 12292
  1279.8 128.2 %copy-start.9 = (bf16[1,512,1024]{2,1,0:T(8,128)(2,1)S(1)}, bf16[1,512,1024]{2,1,0:T(8,128)(2,1)}, u32[]{:S(2)}) copy-start(bf16[1,512,1024]{2,1,0:T(8,128)(2,1)} %reduce-scatter.9.cloned.1.call-done) | copy-start | bytes 3145732
  1279.8 128.2 %copy-start.15 = (bf16[512,1024]{1,0:T(8,128)(2,1)S(1)}, bf16[512,1024]{1,0:T(8,128)(2,1)}, u32[]{:S(2)}) copy-start(bf16[512,1024]{1,0:T(8,128)(2,1)} %param.31) | copy-start | bytes 3145732
  1279.8 128.2 %copy-start.45 = (f32[1024,1]{0,1:T(1,128)S(1)}, f32[1024,1]{0,1:T(1,128)}, u32[]{:S(2)}) copy-start(f32[1024,1]{0,1:T(1,128)} %copy-done.44) | copy-start | bytes 12292
  1279.8 128.2 %copy-start.51 = (f32[512,1]{0,1:T(1,128)S(1)}, f32[512,1]{0,1:T(1,128)}, u32[]{:S(2)}) copy-start(f32[512,1]{0,1:T(1,128)} %copy-done.50) | copy-start | bytes 6148
  1279.8 128.2 %copy-start.54 = (f32[512,1]{0,1:T(1,128)S(1)}, f32[512,1]{0,1:T(1,128)}, u32[]{:S(2)}) copy-start(f32[512,1]{0,1:T(1,128)} %copy-done.53) | copy-start | bytes 6148
  1279.8 128.2 %copy-start.56 = (f32[512,1]{0,1:T(1,128)S(1)}, f32[512,1]{0,1:T(1,128)}, u32[]{:S(2)}) copy-start(f32[512,1]{0,1:T(1,128)} %copy-done.55) | copy-start | bytes 6148
  (49 other events, 222.9 us)
Sparse Core Ops, SparseCore 0:
  26.7 55.0 all-gather.12
  83.7 53.1 all-gather.20
  302.9 71.2 reduce-scatter.8
  376.1 74.5 all-gather.24
  453.1 54.3 all-gather.22
  509.6 80.7 all-gather.14
  592.1 79.2 all-gather.16
  673.0 79.2 all-gather.18
  829.0 69.8 reduce-scatter.12
  910.4 54.3 all-gather.26
  967.2 76.7 reduce-scatter.20
  1046.2 77.2 reduce-scatter.18
  1125.8 77.2 reduce-scatter.22
  1205.4 52.5 reduce-scatter.16
  1261.7 70.9 reduce-scatter.14
  1336.1 71.9 reduce-scatter.10
where the time goes:
time: 1430 us; the launch traced here: 1420 us
  waiting for transfers between devices  558 us (39%)
  local copies, waits for them, and re-layouts  361 us (25%)
  matrix products  229 us (16%)
  blocking collectives  162 us (11%)
  other arithmetic  76.3 us (5%)
  starting transfers between devices  15.8 us (1%)
  between operations  15.6 us (1%)
    all_gather x4, waiting for transfers between devices, full_rows(): return lax.all_gather(spread(local, inner), 't', axis=0, tiled=True)  221 us
    reduce_scatter x4, waiting for transfers between devices, scatter_pieces(): mine = lax.psum_scatter(parts, TP, scatter_dimension=0, tiled=False)  207 us
    dot_general x17, matrix products, dot_f32(): lax.dot_general(left, right, (dims, ((), ())), preferred_element_type=F32)  176 us
    all_to_all x4, blocking collectives, spread(): parts = lax.all_to_all(parts, 'i', 0, 0, tiled=False)  86.1 us
    all_gather x4, waiting for transfers between devices, gather_pieces(): parts = lax.all_gather(piece, TP, axis=0)  84.7 us
    dynamic_update_slice x16, local copies, waits for them, and re-layouts, body(): lax.map(partial(attend_grad, scale=scale), (query_stack, key_stack, value...  61.7 us
    reshape x4, local copies, waits for them, and re-layouts, scatter_pieces(): partial_sum.astype(BF)  57.9 us
    unnamed x163, local copies, waits for them, and re-layouts  56.6 us
  transfers between devices with their start and end apart: 20, of which 16 were waited for; matrix products, arithmetic and copies ran while one was open for 29% of the time, Pallas kernels for 0%

commit v1 on v0

--- a/solution.py
+++ b/solution.py
@@ -242,7 +242,8 @@
     both = jnp.stack([d_gain_one, d_gain_two], 0)
     wide = lax.dynamic_update_slice(jnp.zeros((2, width), F32), both, (0, m_index * width_part))
     small = jnp.concatenate([wide.reshape(-1), d_qgain_part, d_kgain_part])
-    small = lax.psum(small, ALL)
+    shards = lax.all_gather(small, ALL, axis=0, tiled=False)
+    small = shards.sum(axis=0)
     wide = small[: 2 * width].reshape(2, width)
     shard = attn_gain.shape[0]
     own = lax.dynamic_slice(wide, (0, (t_index * inner + i_index) * shard), (2, shard))

time: 1430 us -> 1440 us (level)
  blocking collectives: 162 us -> 197 us
  waiting for transfers between devices: 558 us -> 532 us
    all_gather x0 -> x1, blocking collectives: none -> 75.9 us  [body(): shards = lax.all_gather(small, ALL, axis=0, tiled=False)]
    psum x1 -> x0, blocking collectives: 39.7 us -> none  [body(): small = lax.psum(small, ALL)]
    reduce_scatter x4, waiting for transfers between devices: 207 us -> 180 us  [scatter_pieces(): mine = lax.psum_scatter(parts, TP, scatter_dimension=0, tiled=False)]
    unnamed x163 -> x164, local copies, waits for them, and re-layouts: 56.6 us -> 56.6 us
  transfers between devices with their start and end apart: 20 -> 20, of which waited for: 16 -> 15; matrix products, arithmetic and copies ran while one was open for 29% -> 28% of each run, Pallas kernels for 0% -> 0%
where the time goes in v1:
time: 1440 us; the launch traced here: 1430 us
  waiting for transfers between devices  532 us (37%)
  local copies, waits for them, and re-layouts  361 us (25%)
  matrix products  229 us (16%)
  blocking collectives  197 us (14%)
  other arithmetic  77.6 us (5%)
  starting transfers between devices  15.8 us (1%)
  between operations  15.6 us (1%)
    all_gather x4, waiting for transfers between devices, full_rows(): return lax.all_gather(spread(local, inner), 't', axis=0, tiled=True)  221 us
    reduce_scatter x4, waiting for transfers between devices, scatter_pieces(): mine = lax.psum_scatter(parts, TP, scatter_dimension=0, tiled=False)  180 us
    dot_general x17, matrix products, dot_f32(): lax.dot_general(left, right, (dims, ((), ())), preferred_element_type=F32)  176 us
    all_to_all x4, blocking collectives, spread(): parts = lax.all_to_all(parts, 'i', 0, 0, tiled=False)  86.1 us
    all_gather x4, waiting for transfers between devices, gather_pieces(): parts = lax.all_gather(piece, TP, axis=0)  84.7 us
    all_gather x1, blocking collectives, body(): shards = lax.all_gather(small, ALL, axis=0, tiled=False)  75.9 us
    dynamic_update_slice x16, local copies, waits for them, and re-layouts, body(): lax.map(partial(attend_grad, scale=scale), (query_stack, key_stack, value...  61.7 us
    reshape x4, local copies, waits for them, and re-layouts, scatter_pieces(): partial_sum.astype(BF)  57.9 us
  transfers between devices with their start and end apart: 20, of which 15 were waited for; matrix products, arithmetic and copies ran while one was open for 28% of the time, Pallas kernels for 0%

profile of v1, /device:TPU:0, one launch (start us, length us, event | category | flops | bytes accessed | tf_op | source)
XLA Modules:
  0.0 1429.7 jit_solution(14846242864521315863)
XLA Ops:
  11.3 14.3 all_to_all.40
  27.7 20.5 %all_gather.47 = bf16[2048,2]{0,1:T(2,128)(2,1)S(1)} all-gather(bf16[128,2]{0,1:T(2,128)(2,1)S(1)} %pad_maximum_fusion.6), channel_id=1, replica_groups=mesh['t'=4,'i'=4,'m'=2] {'t','i'}, dimensions={0}, use_global_device_ids=true | all-gather | bytes 8704 | tf_op jit(solution)/shard_map/all_gather | solution.py:153
  50.1 31.7 %all-gather.15.cloned.1.call-done = bf16[2048,640]{0,1:T(8,128)(2,1)} async-done(((bf16[512,640]{0,1:T(8,128)(2,1)}), bf16[2048,640]{0,1:T(8,128)(2,1)}) %all-gather.15.cloned.1.call-update) | async-done | bytes 2621456 | tf_op jit(solution)/shard_map/all_gather | solution.py:114
  81.8 55.0 %all-gather.23.cloned.1.call-done = bf16[4096,1024]{1,0:T(8,128)(2,1)} async-done(((bf16[512,1024]{1,0:T(8,128)(2,1)}), bf16[4096,1024]{1,0:T(8,128)(2,1)}) %all-gather.23.cloned.1.call-update) | async-done | bytes 8388624 | tf_op jit(solution)/shard_map/all_gather | solution.py:87
  142.5 11.3 bitcast_convert_fusion
  153.9 27.7 %copy.137 = f32[4,2,512,1024]{3,1,2,0:T(2,128)S(1)} copy(f32[4,2,512,1024]{3,2,1,0:T(8,128)} %bitcast_convert_fusion) | data formatting | bytes 33554432 | tf_op jit(solution)/shard_map/convert_element_type | solution.py:169
  203.6 16.4 %copy.142 = bf16[4,512,2,1024]{3,2,1,0:T(2,128)(2,1)} copy(bf16[4,512,2,1024]{3,1,2,0:T(8,128)(2,1)} %fusion.58) | data formatting | bytes 16777216 | tf_op jit(solution)/shard_map/mul | solution.py:171
  220.1 14.8 %reshape.765 = bf16[2048,2048,1]{1,0,2:T(8,128)(2,1)} reshape(bf16[4,512,2,1024]{3,2,1,0:T(2,128)(2,1)} %copy.142) | data formatting | bytes 16777216 | tf_op jit(solution)/shard_map/convert_element_type | solution.py:171
  250.3 18.6 %while.26 = (s32[]{:T(128)}, bf16[4,512,4,64]{1,3,2,0:T(8,128)(2,1)}, f32[4,4,512]{2,1,0:T(4,128)}, bf16[4,512,64]{1,2,0:T(8,128)(2,1)S(1)}, pred[4,512,512]{1,2...) while((s32[]{:T(128)}, ...), condition=%wide.region_6.7_spmd, body=%wide.region_3.6_spmd.sunk | while | flops 281147392 | bytes 14617177 | solution.py:185
  278.9 14.5 %reshape.696 = bf16[4,512,2,1024]{3,2,1,0:T(2,128)(2,1)} reshape(bf16[2048,2048]{1,0:T(8,128)(2,1)} %convolution_convert_fusion.2) | data formatting | bytes 16777216 | tf_op jit(solution)/shard_map/reshape | solution.py:94
  303.4 70.8 %reduce-scatter.9.cloned.1.call-done = bf16[1,512,1024]{2,1,0:T(8,128)(2,1)} async-done(((bf16[8,512,1024]{2,1,0:T(8,128)(2,1)}), bf16[1,512,1024]{2,1,0:T(8,128)(2,1)}) %reduce-scatter.9.cloned.1.call-update) | async-done | bytes 1048592 | tf_op jit(solution)/shard_map/reduce_scatter | solution.py:96
  384.2 25.4 %all_to_all.41 = bf16[4,128,1024]{1,2,0:T(8,128)(2,1)S(1)} all-to-all(bf16[4,128,1024]{1,2,0:T(8,128)(2,1)S(1)} %bitcast.453), channel_id=1, replica_groups=mesh['t'=4,'i'=4,'m'=2] {'i'}, dimensions={0} | all-to-all | bytes 2097152 | tf_op jit(solution)/shard_map/all_to_all | solution.py:103
  412.6 28.4 %all_to_all.42 = bf16[4,128,1024]{1,2,0:T(8,128)(2,1)S(1)} all-to-all(bf16[4,128,1024]{1,2,0:T(8,128)(2,1)S(1)} %bitcast.454), channel_id=1, replica_groups=mesh['t'=4,'i'=4,'m'=2] {'i'}, dimensions={0} | all-to-all | bytes 2097152 | tf_op jit(solution)/shard_map/all_to_all | solution.py:103
  442.4 18.0 %all_to_all.43 = bf16[4,128,1024]{1,2,0:T(8,128)(2,1)S(1)} all-to-all(bf16[4,128,1024]{1,2,0:T(8,128)(2,1)} %bitcast.462), channel_id=1, replica_groups=mesh['t'=4,'i'=4,'m'=2] {'i'}, dimensions={0} | all-to-all | bytes 2097152 | tf_op jit(solution)/shard_map/all_to_all | solution.py:103
  461.8 16.7 %copy.155 = bf16[4,2,512,1024]{3,1,2,0:T(2,128)(2,1)} copy(bf16[4,2,512,1024]{3,2,1,0:T(8,128)(2,1)} %bitcast.439) | data formatting | bytes 16777216 | tf_op jit(solution)/shard_map/reshape | solution.py:88
  478.5 10.9 copy.218
  489.4 18.2 %all-gather.25.cloned.1.call-done = bf16[4096,1024]{1,0:T(8,128)(2,1)} async-done(((bf16[512,1024]{1,0:T(8,128)(2,1)}), bf16[4096,1024]{1,0:T(8,128)(2,1)}) %all-gather.25.cloned.1.call-update) | async-done | bytes 8388624 | tf_op jit(solution)/shard_map/all_gather | solution.py:87
  507.5 16.4 %copy.148 = bf16[4,2,512,1024]{3,1,2,0:T(2,128)(2,1)} copy(bf16[4,2,512,1024]{3,2,1,0:T(8,128)(2,1)} %bitcast.444) | data formatting | bytes 16777216 | tf_op jit(solution)/shard_map/reshape | solution.py:88
  524.0 10.2 copy.217
  534.2 56.2 %all-gather.17.cloned.1.call-done = bf16[2048,1024]{1,0:T(8,128)(2,1)} async-done(((bf16[512,1024]{1,0:T(8,128)(2,1)}), bf16[2048,1024]{1,0:T(8,128)(2,1)}) %all-gather.17.cloned.1.call-update) | async-done | bytes 4194320 | tf_op jit(solution)/shard_map/all_gather | solution.py:114
  590.4 14.7 %fusion.116 = f32[2048,1024]{1,0:T(8,128)} fusion(bf16[2048,2048]{1,0:T(8,128)(2,1)} %bitcast.440, bf16[2048,1024]{1,0:T(8,128)(2,1)} %all-gather.17.cloned.1.call-done), kind=kOutput, calls=%fused_computation.219 | convolution fusion | flops 8589934592 | bytes 20971520 | tf_op jit(solution)/shard_map/dot_general | solution.py:16
  605.1 66.3 %all-gather.19.cloned.1.call-done = bf16[2048,1024]{1,0:T(8,128)(2,1)} async-done(((bf16[512,1024]{1,0:T(8,128)(2,1)}), bf16[2048,1024]{1,0:T(8,128)(2,1)}) %all-gather.19.cloned.1.call-update) | async-done | bytes 4194320 | tf_op jit(solution)/shard_map/all_gather | solution.py:114
  671.4 14.4 %fusion.117 = f32[2048,1024]{1,0:T(8,128)} fusion(bf16[2048,2048]{1,0:T(8,128)(2,1)} %bitcast.441, bf16[2048,1024]{1,0:T(8,128)(2,1)} %all-gather.19.cloned.1.call-done), kind=kOutput, calls=%fused_computation.220 | convolution fusion | flops 8589934592 | bytes 20971520 | tf_op jit(solution)/shard_map/dot_general | solution.py:16
  685.8 66.6 %all-gather.21.cloned.1.call-done = bf16[2048,1024]{1,0:T(8,128)(2,1)} async-done(((bf16[512,1024]{1,0:T(8,128)(2,1)}), bf16[2048,1024]{1,0:T(8,128)(2,1)}) %all-gather.21.cloned.1.call-update) | async-done | bytes 4194320 | tf_op jit(solution)/shard_map/all_gather | solution.py:114
  752.4 21.8 %multiply_convert_fusion.2 = (bf16[2048,1024]{1,0:T(8,128)(2,1)}, bf16[2048,1024]{1,0:T(8,128)(2,1)}, bf16[2048,1024]{1,0:T(8,128)(2,1)}) fusion(f32[2048,1024]{1,0:T(8,128)} %fusion.116, f32[2048,1024]{1,0:T(8,128)} %fusion.117, bf16[2048,2048]{1,0:T(8,128)(2,1)} %bitcast.437, bf16[2048,1024]{1,0:T(8,128)(2,1)} %all-gather.21.cloned.1.call-done), kind=kOutput, calls=%fused_computation.70 | convolution fusion | flops 8623489024 | bytes 41943040 | tf_op jit(solution)/shard_map/dot_general | solution.py:16
  774.2 14.4 %fusion.118 = f32[2048,2048]{1,0:T(8,128)} fusion(bf16[2048,1024]{1,0:T(8,128)(2,1)} %get-tuple-element.270, bf16[2048,1024]{1,0:T(8,128)(2,1)S(1)} %copy-done.62), kind=kOutput, calls=%fused_computation.221 | convolution fusion | flops 8589934592 | bytes 25165824 | tf_op jit(solution)/shard_map/dot_general | solution.py:16
  788.6 16.4 %add_convert_fusion = bf16[2048,2048]{1,0:T(8,128)(2,1)} fusion(f32[2048,2048]{1,0:T(8,128)} %fusion.118, bf16[2048,1024]{1,0:T(8,128)(2,1)} %get-tuple-element.269, bf16[2048,1024]{1,0:T(8,128)(2,1)} %all-gather.19.cloned.1.call-done), kind=kOutput, calls=%fused_computation.65 | convolution fusion | flops 8598323200 | bytes 33554432 | tf_op jit(solution)/shard_map/dot_general | solution.py:16
  805.0 14.5 %reshape.710 = bf16[4,512,2,1024]{3,2,1,0:T(2,128)(2,1)} reshape(bf16[2048,2048]{1,0:T(8,128)(2,1)} %add_convert_fusion) | data formatting | bytes 16777216 | tf_op jit(solution)/shard_map/reshape | solution.py:94
  828.9 69.9 %reduce-scatter.13.cloned.1.call-done = bf16[1,512,1024]{2,1,0:T(8,128)(2,1)} async-done(((bf16[8,512,1024]{2,1,0:T(8,128)(2,1)}), bf16[1,512,1024]{2,1,0:T(8,128)(2,1)}) %reduce-scatter.13.cloned.1.call-update) | async-done | bytes 1048592 | tf_op jit(solution)/shard_map/reduce_scatter | solution.py:96
  910.4 14.0 convolution_convert_fusion.3
  924.5 14.0 convolution_convert_fusion.4
  938.8 14.5 %convert_bitcast_fusion = bf16[2048,1024]{0,1:T(8,128)(2,1)} fusion(bf16[2048,1024]{1,0:T(8,128)(2,1)} %get-tuple-element.271, bf16[2048,2048]{1,0:T(8,128)(2,1)} %bitcast.438), kind=kOutput, calls=%fused_computation.77 | convolution fusion | flops 8592031744 | bytes 16777216 | tf_op jit(solution)/shard_map/dot_general | solution.py:16
  953.3 11.5 all-gather.29.cloned.1.call-done
  964.9 16.4 %copy.157 = bf16[4,2,512,1024]{3,1,2,0:T(2,128)(2,1)} copy(bf16[4,2,512,1024]{3,2,1,0:T(8,128)(2,1)} %bitcast.445) | data formatting | bytes 16777216 | tf_op jit(solution)/shard_map/reshape | solution.py:88
  981.3 10.5 copy.220
  1004.3 116.4 %while.27 = (s32[]{:T(128)}, f32[4,512,4,64]{1,0,3,2:T(4,128)}, f32[4,512,64]{1,0,2:T(4,128)}, bf16[4,512,64]{1,2,0:T(8,128)(2,1)}, bf16[4,512,64]{1,2,0:T(8,128...) while((s32[]{:T(128)}, f32[4,512,4,64]{1,0,3,2:T(4,128)}, ...), condition=%wide.region_16.17_spmd, body=%wide.region_14.16_spmd.sunk | while | flops 686979072 | bytes 54259364 | solution.py:216
  1013.1 11.1 dynamic_update_slice.35
  1042.1 11.1 dynamic_update_slice.35
  1071.0 11.1 dynamic_update_slice.35
  1100.0 11.1 dynamic_update_slice.35
  1154.6 14.5 %reshape.721 = bf16[4,512,2,1024]{3,2,1,0:T(2,128)(2,1)} reshape(bf16[2048,2048]{1,0:T(8,128)(2,1)} %convolution_convert_fusion) | data formatting | bytes 16777216 | tf_op jit(solution)/shard_map/reshape | solution.py:94
  1178.5 14.2 convolution_convert_fusion.1
  1192.8 14.5 %reshape.706 = bf16[4,512,2,1024]{3,2,1,0:T(2,128)(2,1)} reshape(bf16[2048,2048]{1,0:T(8,128)(2,1)} %convolution_convert_fusion.1) | data formatting | bytes 16777216 | tf_op jit(solution)/shard_map/reshape | solution.py:94
  1220.4 14.4 %all-to-all-done.6 = bf16[4,128,1024]{2,1,0:T(8,128)(2,1)S(1)} async-done(((bf16[4,128,1024]{2,1,0:T(8,128)(2,1)}), bf16[4,128,1024]{2,1,0:T(8,128)(2,1)S(1)}, u32[]{:S(2)}, u32[]{:S(2)}) %all-to-all-start.6) | async-done | bytes 1048608 | tf_op jit(solution)/shard_map/all_to_all | solution.py:109
  1240.7 12.0 all-to-all-done.5
  1260.1 10.6 all-to-all-done.7
  1293.1 39.7 %reduce-scatter.15.cloned.1.call-done = bf16[1,512,1024]{2,1,0:T(8,128)(2,1)} async-done(((bf16[8,512,1024]{2,1,0:T(8,128)(2,1)}), bf16[1,512,1024]{2,1,0:T(8,128)(2,1)}) %reduce-scatter.15.cloned.1.call-update) | async-done | bytes 1048592 | tf_op jit(solution)/shard_map/reduce_scatter | solution.py:96
  1335.0 75.9 %all-gather.5 = f32[32,1,4224]{2,1,0:T(1,128)} all-gather(f32[1,1,4224]{2,1,0:T(1,128)S(1)} %reshape.756), channel_id=6, replica_groups=mesh['t'=4,'i'=4,'m'=2] {'t','i','m'}, dimensions={0}, use_global_device_ids=true | all-gather | bytes 557568 | tf_op jit(solution)/shard_map/all_gather | solution.py:245
  (383 shorter events, 315.4 us)
Async XLA Ops:
  7.2 20.2 %copy-start = (s32[16,2]{0,1:T(2,128)S(1)}, s32[16,2]{0,1:T(2,128)}, u32[]{:S(2)}) copy-start(s32[16,2]{0,1:T(2,128)} %param.19) | copy-start | bytes 388
  7.2 20.4 %copy-start.63 = (bf16[64]{0:T(256)(128)(2,1)S(1)}, bf16[64]{0:T(256)(128)(2,1)}, u32[]{:S(2)}) copy-start(bf16[64]{0:T(256)(128)(2,1)} %param.25) | copy-start | bytes 388
  7.2 20.4 %copy-start.65 = (bf16[128]{0:T(256)(128)(2,1)S(1)}, bf16[128]{0:T(256)(128)(2,1)}, u32[]{:S(2)}) copy-start(bf16[128]{0:T(256)(128)(2,1)} %param.20) | copy-start | bytes 772
  7.2 20.4 %copy-start.64 = (bf16[128]{0:T(256)(128)(2,1)S(1)}, bf16[128]{0:T(256)(128)(2,1)}, u32[]{:S(2)}) copy-start(bf16[128]{0:T(256)(128)(2,1)} %param.27) | copy-start | bytes 772
  7.2 40.9 %copy-start.66 = (bf16[64]{0:T(256)(128)(2,1)S(1)}, bf16[64]{0:T(256)(128)(2,1)}, u32[]{:S(2)}) copy-start(bf16[64]{0:T(256)(128)(2,1)} %param.24) | copy-start | bytes 388
  7.2 74.5 %all-gather.15.cloned.1.call-start = ((), (), s32[]{:S(2)}) async-start(), calls=%async_computation.16 | async-start | bytes 3276800 | tf_op jit(solution)/shard_map/all_gather | solution.py:114
  26.6 110.3 %all-gather.23.cloned.1.call-start = ((), (), s32[]{:S(2)}) async-start(), calls=%async_computation.28 | async-start | bytes 9437184 | tf_op jit(solution)/shard_map/all_gather | solution.py:87
  27.3 346.9 %reduce-scatter.9.cloned.1.call-start = ((), (), s32[]{:S(2)}) async-start(), calls=%async_computation.17 | async-start | bytes 9437184 | tf_op jit(solution)/shard_map/reduce_scatter | solution.py:96
  27.6 213.8 %copy-start.60 = (f32[64]{0:T(128)}, f32[64]{0:T(128)S(1)}, u32[]{:S(2)}) copy-start(f32[64]{0:T(128)S(1)} %convert_element_type.239) | copy-start | bytes 772
  48.2 196.1 %copy-start.58 = (f32[64]{0:T(128)}, f32[64]{0:T(128)S(1)}, u32[]{:S(2)}) copy-start(f32[64]{0:T(128)S(1)} %convert_element_type.247) | copy-start | bytes 772
  49.2 138.4 %copy-start.48 = (f32[2048,1]{0,1:T(1,128)}, f32[2048,1]{0,1:T(1,128)S(1)}, u32[]{:S(2)}) copy-start(f32[2048,1]{0,1:T(1,128)S(1)} %get-tuple-element.297) | copy-start | bytes 24580
  193.4 48.0 %copy-start.11 = (f32[2048,64]{0,1:T(8,128)}, f32[2048,64]{0,1:T(8,128)S(1)}, u32[]{:S(2)}) copy-start(f32[2048,64]{0,1:T(8,128)S(1)} %get-tuple-element.306) | copy-start | bytes 1572868
  194.0 47.4 %copy-start.40 = (f32[2048]{0:T(1024)}, f32[2048]{0:T(1024)S(1)}, u32[]{:S(2)}) copy-start(f32[2048]{0:T(1024)S(1)} %fusion.102) | copy-start | bytes 24580
  302.7 71.5 %copy-start.4 = (bf16[512,1024]{1,0:T(8,128)(2,1)S(1)}, bf16[512,1024]{1,0:T(8,128)(2,1)}, u32[]{:S(2)}) copy-start(bf16[512,1024]{1,0:T(8,128)(2,1)} %param.18) | copy-start | bytes 3145732
  302.7 80.8 %copy-start.32 = (bf16[128,4096]{1,0:T(8,128)(2,1)S(1)}, bf16[128,4096]{1,0:T(8,128)(2,1)}, u32[]{:S(2)}) copy-start(bf16[128,4096]{1,0:T(8,128)(2,1)} %param.28) | copy-start | bytes 3145732
  302.7 159.0 %all-gather.27.cloned.1.call-start = ((), (), s32[]{:S(2)}) async-start(), calls=%async_computation.30 | async-start | bytes 9437184 | tf_op jit(solution)/shard_map/all_gather | solution.py:87
  303.3 204.2 %all-gather.25.cloned.1.call-start = ((), (), s32[]{:S(2)}) async-start(), calls=%async_computation.29 | async-start | bytes 9437184 | tf_op jit(solution)/shard_map/all_gather | solution.py:87
  303.4 603.3 %copy-start.44 = (f32[1024,1]{0,1:T(1,128)}, f32[1024,1]{0,1:T(1,128)S(1)}, u32[]{:S(2)}) copy-start(f32[1024,1]{0,1:T(1,128)S(1)} %dynamic-slice_convert_fusion) | copy-start | bytes 12292
  380.8 525.9 %copy-start.50 = (f32[512,1]{0,1:T(1,128)}, f32[512,1]{0,1:T(1,128)S(1)}, u32[]{:S(2)}) copy-start(f32[512,1]{0,1:T(1,128)S(1)} %get-tuple-element.264) | copy-start | bytes 6148
  380.8 525.9 %copy-start.53 = (f32[512,1]{0,1:T(1,128)}, f32[512,1]{0,1:T(1,128)S(1)}, u32[]{:S(2)}) copy-start(f32[512,1]{0,1:T(1,128)S(1)} %get-tuple-element.263) | copy-start | bytes 6148
  383.4 207.0 %all-gather.17.cloned.1.call-start = ((), (), s32[]{:S(2)}) async-start(), calls=%async_computation.18 | async-start | bytes 5242880 | tf_op jit(solution)/shard_map/all_gather | solution.py:114
  410.9 260.5 %all-gather.19.cloned.1.call-start = ((), (), s32[]{:S(2)}) async-start(), calls=%async_computation.19 | async-start | bytes 5242880 | tf_op jit(solution)/shard_map/all_gather | solution.py:114
  442.3 310.0 %all-gather.21.cloned.1.call-start = ((), (), s32[]{:S(2)}) async-start(), calls=%async_computation.20 | async-start | bytes 5242880 | tf_op jit(solution)/shard_map/all_gather | solution.py:114
  461.7 437.2 %reduce-scatter.13.cloned.1.call-start = ((), (), s32[]{:S(2)}) async-start(), calls=%async_computation.22 | async-start | bytes 9437184 | tf_op jit(solution)/shard_map/reduce_scatter | solution.py:96
  752.4 21.8 %copy-start.62 = (bf16[2048,1024]{1,0:T(8,128)(2,1)S(1)}, bf16[2048,1024]{1,0:T(8,128)(2,1)}, u32[]{:S(2)}) copy-start(bf16[2048,1024]{1,0:T(8,128)(2,1)} %all-gather.17.cloned.1.call-done) | copy-start | bytes 12582916
  828.8 70.0 %copy-start.8 = (bf16[1,512,1024]{2,1,0:T(8,128)(2,1)S(1)}, bf16[1,512,1024]{2,1,0:T(8,128)(2,1)}, u32[]{:S(2)}) copy-start(bf16[1,512,1024]{2,1,0:T(8,128)(2,1)} %reduce-scatter.9.cloned.1.call-done) | copy-start | bytes 3145732
  828.8 78.4 %copy-start.14 = (bf16[512,1024]{1,0:T(8,128)(2,1)S(1)}, bf16[512,1024]{1,0:T(8,128)(2,1)}, u32[]{:S(2)}) copy-start(bf16[512,1024]{1,0:T(8,128)(2,1)} %param.31) | copy-start | bytes 3145732
  828.9 136.0 %all-gather.29.cloned.1.call-start = ((), (), s32[]{:S(2)}) async-start(), calls=%async_computation.31 | async-start | bytes 9437184 | tf_op jit(solution)/shard_map/all_gather | solution.py:87
  910.3 306.3 %reduce-scatter.21.cloned.1.call-start = ((), (), s32[]{:S(2)}) async-start(), calls=%async_computation.26 | async-start | bytes 5242880 | tf_op jit(solution)/shard_map/reduce_scatter | solution.py:118
  924.5 295.9 %reduce-scatter.19.cloned.1.call-start = ((), (), s32[]{:S(2)}) async-start(), calls=%async_computation.25 | async-start | bytes 5242880 | tf_op jit(solution)/shard_map/reduce_scatter | solution.py:118
  938.5 299.8 %reduce-scatter.23.cloned.1.call-start = ((), (), s32[]{:S(2)}) async-start(), calls=%async_computation.27 | async-start | bytes 5242880 | tf_op jit(solution)/shard_map/reduce_scatter | solution.py:118
  953.3 304.8 %reduce-scatter.17.cloned.1.call-start = ((), (), s32[]{:S(2)}) async-start(), calls=%async_computation.24 | async-start | bytes 3276800 | tf_op jit(solution)/shard_map/reduce_scatter | solution.py:118
  1145.6 187.2 %reduce-scatter.15.cloned.1.call-start = ((), (), s32[]{:S(2)}) async-start(), calls=%async_computation.23 | async-start | bytes 9437184 | tf_op jit(solution)/shard_map/reduce_scatter | solution.py:96
  1178.5 239.9 %reduce-scatter.11.cloned.1.call-start = ((), (), s32[]{:S(2)}) async-start(), calls=%async_computation.21 | async-start | bytes 9437184 | tf_op jit(solution)/shard_map/reduce_scatter | solution.py:96
  1216.7 39.6 %copy-start.49 = (f32[2048,1]{0,1:T(1,128)S(1)}, f32[2048,1]{0,1:T(1,128)}, u32[]{:S(2)}) copy-start(f32[2048,1]{0,1:T(1,128)} %copy-done.48) | copy-start | bytes 24580
  1216.7 39.6 %copy-start.52 = (f32[1,1,4,512]{3,2,1,0:T(4,128)S(1)}, f32[1,1,4,512]{3,2,1,0:T(4,128)}, u32[]{:S(2)}) copy-start(f32[1,1,4,512]{3,2,1,0:T(4,128)} %get-tuple-element.293) | copy-start | bytes 24580
  1216.7 18.1 %all-to-all-start.6 = ((bf16[4,128,1024]{2,1,0:T(8,128)(2,1)}), bf16[4,128,1024]{2,1,0:T(8,128)(2,1)S(1)}, u32[]{:S(2)}, u32[]{:S(2)}) async-start(bf16[4,128,1024]{2,1,0:T(8,128)(2,1)} %bitcast.464), calls=%async_computation.13 | async-start | bytes 2097152 | tf_op jit(solution)/shard_map/all_to_all | solution.py:109
  1234.8 18.0 %all-to-all-start.5 = ((bf16[4,128,1024]{2,1,0:T(8,128)(2,1)}), bf16[4,128,1024]{2,1,0:T(8,128)(2,1)S(1)}, u32[]{:S(2)}, u32[]{:S(2)}) async-start(bf16[4,128,1024]{2,1,0:T(8,128)(2,1)} %bitcast.463), calls=%async_computation.11 | async-start | bytes 2097152 | tf_op jit(solution)/shard_map/all_to_all | solution.py:109
  1252.7 18.0 %all-to-all-start.7 = ((bf16[4,128,1024]{1,2,0:T(8,128)(2,1)}), bf16[4,128,1024]{1,2,0:T(8,128)(2,1)S(1)}, u32[]{:S(2)}, u32[]{:S(2)}) async-start(bf16[4,128,1024]{1,2,0:T(8,128)(2,1)} %copy_bitcast_fusion), calls=%async_computation.15 | async-start | bytes 2097152 | tf_op jit(solution)/shard_map/all_to_all | solution.py:109
  1270.7 14.5 %all-to-all-start.4 = ((bf16[4,128,640]{1,2,0:T(8,128)(2,1)}), bf16[4,128,640]{1,2,0:T(8,128)(2,1)}, u32[]{:S(2)}, u32[]{:S(2)}) async-start(bf16[4,128,640]{1,2,0:T(8,128)(2,1)} %copy_bitcast_fusion.3), calls=%async_computation.9 | async-start | bytes 1310720 | tf_op jit(solution)/shard_map/all_to_all | solution.py:109
  1278.4 54.4 %copy-start.5 = (bf16[512,1024]{1,0:T(8,128)(2,1)S(1)}, bf16[512,1024]{1,0:T(8,128)(2,1)}, u32[]{:S(2)}) copy-start(bf16[512,1024]{1,0:T(8,128)(2,1)} %param.18) | copy-start | bytes 3145732
  1279.8 55.1 %copy-start.57 = (f32[1024]{0:T(1024)S(1)}, f32[1024]{0:T(1024)}, u32[]{:S(2)}) copy-start(f32[1024]{0:T(1024)} %get-tuple-element.219) | copy-start | bytes 12292
  1287.5 130.9 %copy-start.9 = (bf16[1,512,1024]{2,1,0:T(8,128)(2,1)S(1)}, bf16[1,512,1024]{2,1,0:T(8,128)(2,1)}, u32[]{:S(2)}) copy-start(bf16[1,512,1024]{2,1,0:T(8,128)(2,1)} %reduce-scatter.9.cloned.1.call-done) | copy-start | bytes 3145732
  1287.5 130.9 %copy-start.15 = (bf16[512,1024]{1,0:T(8,128)(2,1)S(1)}, bf16[512,1024]{1,0:T(8,128)(2,1)}, u32[]{:S(2)}) copy-start(bf16[512,1024]{1,0:T(8,128)(2,1)} %param.31) | copy-start | bytes 3145732
  1287.5 130.9 %copy-start.45 = (f32[1024,1]{0,1:T(1,128)S(1)}, f32[1024,1]{0,1:T(1,128)}, u32[]{:S(2)}) copy-start(f32[1024,1]{0,1:T(1,128)} %copy-done.44) | copy-start | bytes 12292
  1287.5 130.9 %copy-start.51 = (f32[512,1]{0,1:T(1,128)S(1)}, f32[512,1]{0,1:T(1,128)}, u32[]{:S(2)}) copy-start(f32[512,1]{0,1:T(1,128)} %copy-done.50) | copy-start | bytes 6148
  1287.5 131.0 %copy-start.54 = (f32[512,1]{0,1:T(1,128)S(1)}, f32[512,1]{0,1:T(1,128)}, u32[]{:S(2)}) copy-start(f32[512,1]{0,1:T(1,128)} %copy-done.53) | copy-start | bytes 6148
  1287.5 131.0 %copy-start.56 = (f32[512,1]{0,1:T(1,128)S(1)}, f32[512,1]{0,1:T(1,128)}, u32[]{:S(2)}) copy-start(f32[512,1]{0,1:T(1,128)} %copy-done.55) | copy-start | bytes 6148
  (49 other events, 223.0 us)
Sparse Core Ops, SparseCore 0:
  26.7 55.0 all-gather.14
  83.7 53.1 all-gather.22
  302.9 71.2 reduce-scatter.8
  376.1 74.5 all-gather.26
  453.1 54.3 all-gather.24
  509.6 80.7 all-gather.16
  592.1 79.2 all-gather.18
  673.0 79.2 all-gather.20
  829.0 69.8 reduce-scatter.12
  910.4 54.3 all-gather.28
  967.2 76.7 reduce-scatter.20
  1046.2 77.2 reduce-scatter.18
  1125.8 77.2 reduce-scatter.22
  1205.4 52.5 reduce-scatter.16
  1261.7 70.9 reduce-scatter.14
  1336.1 76.1 reduce-scatter.10
